TPU v7x, 32 devices: a whole 2x2x4 slice. The times are simulated.
32 devices in a mesh: seq: 2 (over core), narrow: 4 (over y, x), wide: 4 (over z).
Axes of the slice: x: 2, y: 2, z: 4, core: 2. Of those that a mesh axis runs over, the one named last changes fastest.
Arguments:
- tokens: bfloat16 [8192, 2048], P('seq', 'narrow'), may hold values from -6 to 6
- attn_gain: float32 [2048], P('narrow'), may hold values from 0.5 to 1.5
- w_query: bfloat16 [2048, 2048], P('narrow', 'wide'), may hold values from -0.125 to 0.125
- w_key: bfloat16 [2048, 512], P('narrow', 'wide'), may hold values from -0.125 to 0.125
- w_value: bfloat16 [2048, 512], P('narrow', 'wide'), may hold values from -0.125 to 0.125
- w_out: bfloat16 [2048, 2048], P('wide', 'narrow'), may hold values from -2 to 2
- ffn_gain: float32 [2048], P('narrow'), may hold values from 0.5 to 1.5
- w_gate: bfloat16 [2048, 8192], P('narrow', 'wide'), may hold values from -0.125 to 0.125
- w_up: bfloat16 [2048, 8192], P('narrow', 'wide'), may hold values from -0.125 to 0.125
- w_down: bfloat16 [8192, 2048], P('wide', 'narrow'), may hold values from -0.0625 to 0.0625
- segment_ids: int32 [8192], replicated, may hold values from 0 to 2, as said below
- token_mask: int32 [8192], replicated, may hold values from 0 to 1, as said below
- out_grad: bfloat16 [8192, 2048], P('seq', 'narrow'), may hold values from -6 to 6
Outputs:
- result: bfloat16 [8192, 2048], P('seq', 'narrow')
- input_grad: float32 [8192, 2048], P('seq', 'narrow')
- grad_attn_gain: float32 [2048], P('narrow')
- grad_w_query: float32 [2048, 2048], P('narrow', 'wide')
- grad_w_key: float32 [2048, 512], P('narrow', 'wide')
- grad_w_value: float32 [2048, 512], P('narrow', 'wide')
- grad_w_out: float32 [2048, 2048], P('wide', 'narrow')
- grad_ffn_gain: float32 [2048], P('narrow')
- grad_w_gate: float32 [2048, 8192], P('narrow', 'wide')
- grad_w_up: float32 [2048, 8192], P('narrow', 'wide')
- grad_w_down: float32 [8192, 2048], P('wide', 'narrow')
Inputs may be any that keep to these rules, and one draw needn't show every extreme that they name: `segment_ids`: the pack holds three sequences in order, ids 0, 1, 2, never falling: the first and the last hold 2 to 256 positions each, the middle one all the rest. `token_mask`: padding is the last positions of each sequence: 1 to 255 of the middle one; of the first and the last, one or more and fewer than the sequence's length; the first position of each sequence is a real token.
All inputs are finite; a program needn't handle non-finite values.
Results may differ from a plain program's by a relative error of at most 0.018.
Values may be sent and summed in bfloat16 or wider, within the bound.
A program may use at most 384 MiB of HBM per device.

v0:
```python
import jax
import jax.numpy as jnp
from jax import lax
from jax.sharding import PartitionSpec as P

D = 2048
HD = 64
EPS = 1e-05
THETA = 500000.0
NEG = -1e30


def positions(segment_ids):
    token_index = jnp.arange(segment_ids.shape[0], dtype=jnp.int32)
    seg_first = jnp.concatenate([jnp.ones((1,), dtype=bool), segment_ids[1:] != segment_ids[:-1]])
    seg_start = lax.cummax(jnp.where(seg_first, token_index, jnp.zeros_like(token_index)), axis=0)
    return token_index - seg_start


def rotation(token_pos):
    half_dim = HD // 2
    frequency = THETA ** (-2.0 * jnp.arange(half_dim, dtype=jnp.float32) / HD)
    angles = token_pos.astype(jnp.float32)[:, None] * frequency[None, :]
    cosine_table = jnp.concatenate([jnp.cos(angles), jnp.cos(angles)], axis=1)
    sine_table = jnp.concatenate([jnp.sin(angles), jnp.sin(angles)], axis=1)
    return (cosine_table, sine_table)


def rotate(vectors, cosine_table, sine_table, turn_sign):
    half_dim = HD // 2
    turned = jnp.concatenate([-vectors[..., half_dim:], vectors[..., :half_dim]], axis=-1)
    return vectors * cosine_table[:, None, :] + turn_sign * turned * sine_table[:, None, :]


def narrow_total(values):
    return lax.psum(values, "narrow")


def wide_total(values):
    return lax.psum(values, "wide")


def gather_rows(values):
    return lax.all_gather(values, "narrow", axis=0, tiled=True)


def rms_norm(values):
    squares = narrow_total(jnp.sum(values * values, axis=1))
    row_scale = lax.rsqrt(squares / D + EPS)
    return (values * row_scale[:, None], row_scale)


def norm_back(grad_h, normed, row_scale, gain_vec):
    grad_normed = grad_h * gain_vec[None, :]
    inner_sum = narrow_total(jnp.sum(grad_normed * normed, axis=1))
    grad_input = row_scale[:, None] * (grad_normed - normed * (inner_sum / D)[:, None])
    return (grad_input, jnp.sum(grad_h * normed, axis=0))


def sum_rows(left_side, weight, product_kind):

    def term_rows():
        if product_kind == "flip":
            return lax.dot_general(
                left_side, weight, (((1,), (1,)), ((), ())), preferred_element_type=jnp.float32
            )
        return jnp.dot(left_side, weight, preferred_element_type=jnp.float32)

    return lax.psum_scatter(term_rows(), "narrow", scatter_dimension=0, tiled=True)


def back_rows(grad_rows, weight, inputs):
    shard_piece = lax.all_gather(grad_rows, "narrow", axis=0, tiled=True)
    product = lax.dot_general(
        shard_piece, weight, (((1,), (1,)), ((), ())), preferred_element_type=jnp.float32
    )
    weight_grad = lax.dot_general(
        inputs, shard_piece, (((0,), (0,)), ((), ())), preferred_element_type=jnp.float32
    )
    return (product, weight_grad)


def body(
    tokens,
    attn_gain,
    w_query,
    w_key,
    w_value,
    w_out,
    ffn_gain,
    w_gate,
    w_up,
    w_down,
    segment_ids,
    token_mask,
    out_grad,
):
    narrow_count = lax.axis_size("narrow")
    tok_count = tokens.shape[0]
    quarter = tok_count // narrow_count
    total_tokens = segment_ids.shape[0]
    seq_index = lax.axis_index("seq")
    narrow_index = lax.axis_index("narrow")
    q_width = w_query.shape[1]
    kv_width = w_key.shape[1]
    q_heads = q_width // HD
    kv_heads = kv_width // HD
    group_size = q_heads // kv_heads
    ff_width = w_gate.shape[1]
    score_scale = HD ** (-0.5)
    cosine_all, sine_all = rotation(positions(segment_ids))
    own_first = seq_index * tok_count + narrow_index * quarter
    own_index = own_first + jnp.arange(quarter, dtype=jnp.int32)
    cosine_table = lax.dynamic_slice_in_dim(cosine_all, own_first, quarter, 0)
    sine_table = lax.dynamic_slice_in_dim(sine_all, own_first, quarter, 0)
    own_segment = lax.dynamic_slice_in_dim(segment_ids, own_first, quarter, 0)
    key_index = jnp.arange(total_tokens, dtype=jnp.int32)
    allowed = (
        (own_segment[:, None] == segment_ids[None, :])
        & (key_index[None, :] <= own_index[:, None])
        & (token_mask[None, :] == 1)
    )
    row_valid = lax.dynamic_slice_in_dim(token_mask, seq_index * tok_count, tok_count, 0)
    grad_low = jnp.where(row_valid[:, None] == 1, out_grad, jnp.zeros_like(out_grad))
    grad_float = grad_low.astype(jnp.float32)
    x_float = tokens.astype(jnp.float32)
    normed_one, scale_one = rms_norm(x_float)
    h_one = (normed_one * attn_gain[None, :]).astype(jnp.bfloat16)
    w_qkv = jnp.concatenate([w_query, w_key, w_value], axis=1)
    qkv_lin = sum_rows(h_one, w_qkv, "plain")
    query_rot = rotate(
        qkv_lin[:, :q_width].reshape(quarter, q_heads, HD), cosine_table, sine_table, 1.0
    ).astype(jnp.bfloat16)
    key_rot = rotate(
        qkv_lin[:, q_width : q_width + kv_width].reshape(quarter, kv_heads, HD),
        cosine_table,
        sine_table,
        1.0,
    ).astype(jnp.bfloat16)
    value_low = qkv_lin[:, q_width + kv_width :].astype(jnp.bfloat16)
    kv_local = jnp.concatenate([key_rot.reshape(quarter, kv_width), value_low], axis=1)
    kv_all = lax.all_gather(kv_local, ("seq", "narrow"), axis=0, tiled=True)
    keys_all = kv_all[:, :kv_width].reshape(total_tokens, kv_heads, HD)
    values_all = kv_all[:, kv_width:].reshape(total_tokens, kv_heads, HD)
    query_heads = jnp.transpose(query_rot, (1, 0, 2))
    head_ids = jnp.arange(q_heads, dtype=jnp.int32)

    def head_scores(query_one, head_id):
        kv_id = head_id // group_size
        key_one = lax.dynamic_index_in_dim(keys_all, kv_id, 1, keepdims=False)
        value_one = lax.dynamic_index_in_dim(values_all, kv_id, 1, keepdims=False)
        scores = (
            lax.dot_general(
                query_one, key_one, (((1,), (1,)), ((), ())), preferred_element_type=jnp.float32
            )
            * score_scale
        )
        return (jnp.where(allowed, scores, NEG), key_one, value_one)

    def head_forward(packed):
        query_one, head_id = packed
        scores, key_one, value_one = head_scores(query_one, head_id)
        row_top = jnp.max(scores, axis=1, keepdims=True)
        log_total = row_top + jnp.log(jnp.sum(jnp.exp(scores - row_top), axis=1, keepdims=True))
        prob_low = jnp.exp(scores - log_total).astype(jnp.bfloat16)
        return (jnp.dot(prob_low, value_one, preferred_element_type=jnp.float32), log_total[:, 0])

    head_out, log_totals = lax.map(head_forward, (query_heads, head_ids))
    attn_heads = jnp.transpose(head_out, (1, 0, 2)).reshape(quarter, q_width).astype(jnp.bfloat16)
    attn_all = gather_rows(attn_heads)
    middle = x_float + wide_total(jnp.dot(attn_all, w_out, preferred_element_type=jnp.float32))
    normed_two, scale_two = rms_norm(middle)
    h_two = (normed_two * ffn_gain[None, :]).astype(jnp.bfloat16)
    w_gate_up = jnp.concatenate([w_gate, w_up], axis=1)
    gate_up = sum_rows(h_two, w_gate_up, "plain")
    gate_lin = gate_up[:, :ff_width]
    up_lin = gate_up[:, ff_width:]
    gate_sig = jax.nn.sigmoid(gate_lin)
    act_low = (gate_lin * gate_sig * up_lin).astype(jnp.bfloat16)
    act_all = gather_rows(act_low)
    down_sum = wide_total(jnp.dot(act_all, w_down, preferred_element_type=jnp.float32))
    result = (middle + down_sum).astype(jnp.bfloat16)
    grad_w_down = lax.dot_general(
        act_all, grad_low, (((0,), (0,)), ((), ())), preferred_element_type=jnp.float32
    )
    act_grad = sum_rows(grad_low, w_down, "flip")
    gate_grad = act_grad * up_lin * gate_sig * (1.0 + gate_lin * (1.0 - gate_sig))
    up_grad = act_grad * gate_lin * gate_sig
    gate_up_grad = jnp.concatenate([gate_grad, up_grad], axis=1).astype(jnp.bfloat16)
    middle_part, grad_gate_up = back_rows(gate_up_grad, w_gate_up, h_two)
    middle_norm_grad, grad_ffn_gain = norm_back(
        wide_total(middle_part), normed_two, scale_two, ffn_gain
    )
    middle_grad = grad_float + middle_norm_grad
    attn_grad_low = middle_grad.astype(jnp.bfloat16)
    grad_w_out = lax.dot_general(
        attn_all, attn_grad_low, (((0,), (0,)), ((), ())), preferred_element_type=jnp.float32
    )
    heads_grad = sum_rows(attn_grad_low, w_out, "flip").astype(jnp.bfloat16)
    heads_grad_split = jnp.transpose(heads_grad.reshape(quarter, q_heads, HD), (1, 0, 2))

    def head_backward(packed):
        query_one, grad_one, log_total, head_id = packed
        scores, key_one, value_one = head_scores(query_one, head_id)
        attn_prob = jnp.exp(scores - log_total[:, None])
        prob_low = attn_prob.astype(jnp.bfloat16)
        prob_grad = lax.dot_general(
            grad_one, value_one, (((1,), (1,)), ((), ())), preferred_element_type=jnp.float32
        )
        inner_sum = jnp.sum(attn_prob * prob_grad, axis=1, keepdims=True)
        score_grad = (attn_prob * (prob_grad - inner_sum)).astype(jnp.bfloat16)
        query_grad = jnp.dot(score_grad, key_one, preferred_element_type=jnp.float32) * score_scale
        key_grad = (
            lax.dot_general(
                score_grad, query_one, (((0,), (0,)), ((), ())), preferred_element_type=jnp.float32
            )
            * score_scale
        )
        value_grad = lax.dot_general(
            prob_low, grad_one, (((0,), (0,)), ((), ())), preferred_element_type=jnp.float32
        )
        return (query_grad, key_grad, value_grad)

    query_grads, key_grads, value_grads = lax.map(
        head_backward, (query_heads, heads_grad_split, log_totals, head_ids)
    )
    key_sum = jnp.sum(key_grads.reshape(kv_heads, group_size, total_tokens, HD), axis=1)
    value_sum = jnp.sum(value_grads.reshape(kv_heads, group_size, total_tokens, HD), axis=1)
    kv_grad_all = jnp.concatenate(
        [
            jnp.transpose(key_sum, (1, 0, 2)).reshape(total_tokens, kv_width),
            jnp.transpose(value_sum, (1, 0, 2)).reshape(total_tokens, kv_width),
        ],
        axis=1,
    )
    kv_grad = lax.psum_scatter(
        kv_grad_all.astype(jnp.bfloat16), ("seq", "narrow"), scatter_dimension=0, tiled=True
    ).astype(jnp.float32)
    query_back = rotate(
        jnp.transpose(query_grads, (1, 0, 2)), cosine_table, sine_table, -1.0
    ).reshape(quarter, q_width)
    key_back = rotate(
        kv_grad[:, :kv_width].reshape(quarter, kv_heads, HD), cosine_table, sine_table, -1.0
    ).reshape(quarter, kv_width)
    qkv_grad = jnp.concatenate([query_back, key_back, kv_grad[:, kv_width:]], axis=1).astype(
        jnp.bfloat16
    )
    first_part, grad_qkv = back_rows(qkv_grad, w_qkv, h_one)
    input_part, grad_attn_gain = norm_back(wide_total(first_part), normed_one, scale_one, attn_gain)
    input_grad = middle_grad + input_part
    summed = (
        lax.psum(grad_attn_gain.astype(jnp.bfloat16), "seq").astype(jnp.float32),
        lax.psum(grad_qkv.astype(jnp.bfloat16), "seq").astype(jnp.float32),
        lax.psum(grad_w_out.astype(jnp.bfloat16), "seq").astype(jnp.float32),
        lax.psum(grad_ffn_gain.astype(jnp.bfloat16), "seq").astype(jnp.float32),
        lax.psum(grad_gate_up.astype(jnp.bfloat16), "seq").astype(jnp.float32),
        lax.psum(grad_w_down.astype(jnp.bfloat16), "seq").astype(jnp.float32),
    )
    qkv_total = summed[1]
    gate_up_total = summed[4]
    return (
        result,
        input_grad,
        summed[0],
        qkv_total[:, :q_width],
        qkv_total[:, q_width : q_width + kv_width],
        qkv_total[:, q_width + kv_width :],
        summed[2],
        summed[3],
        gate_up_total[:, :ff_width],
        gate_up_total[:, ff_width:],
        summed[5],
    )


def solution(mesh):
    return jax.shard_map(
        body,
        mesh=mesh,
        in_specs=(
            P("seq", "narrow"),
            P("narrow"),
            P("narrow", "wide"),
            P("narrow", "wide"),
            P("narrow", "wide"),
            P("wide", "narrow"),
            P("narrow"),
            P("narrow", "wide"),
            P("narrow", "wide"),
            P("wide", "narrow"),
            P(),
            P(),
            P("seq", "narrow"),
        ),
        out_specs=(
            P("seq", "narrow"),
            P("seq", "narrow"),
            P("narrow"),
            P("narrow", "wide"),
            P("narrow", "wide"),
            P("narrow", "wide"),
            P("wide", "narrow"),
            P("narrow"),
            P("narrow", "wide"),
            P("narrow", "wide"),
            P("wide", "narrow"),
        ),
        check_vma=False,
    )
```

profile of v0, /device:TPU:0, one launch (start us, length us, event | category | flops | bytes accessed | tf_op | source)
XLA Modules:
  0.0 4983.6 jit_solution(15209267365387991906)
XLA Ops:
  51.3 111.1 %reduce-scatter.5.cloned.1.call-done = f32[1024,768]{1,0:T(8,128)} async-done(((f32[4096,768]{1,0:T(8,128)}), f32[1024,768]{1,0:T(8,128)}) %reduce-scatter.5.cloned.1.call-update) | async-done | bytes 3145744 | tf_op jit(solution)/shard_map/reduce_scatter | solution.py:69
  217.7 410.5 %while.34 = (s32[]{:T(128)}, bf16[8,1024,64]{1,2,0:T(8,128)(2,1)S(1)}, f32[8,1024]{1,0:T(8,128)}, bf16[8,1024,64]{2,1,0:T(8,128)(2,1)}, s32[8]{0:T(128)S(1)}, /*...) while((s32[]{:T(128)}, ...), condition=%wide.region_8.9_spmd.clone.clone, body=%wide.region_5.8_spmd.clone.sunk.clone | while | flops 2239757312 | bytes 111760208 | solution.py:168
  629.6 52.4 %all-gather.8.cloned.1.call-done = bf16[4096,512]{0,1:T(8,128)(2,1)} async-done(((bf16[1024,512]{0,1:T(8,128)(2,1)}), bf16[4096,512]{0,1:T(8,128)(2,1)}) %all-gather.8.cloned.1.call-update) | async-done | bytes 4194320 | tf_op jit(solution)/shard_map/all_gather | solution.py:44
  714.4 266.7 %all-reduce.10.cloned.1.call-done = f32[4096,512]{1,0:T(8,128)} async-done(((f32[4096,512]{1,0:T(8,128)}), f32[4096,512]{1,0:T(8,128)}) %all-reduce.10.cloned.1.call-update) | async-done | bytes 8388624 | tf_op jit(solution)/shard_map/psum | solution.py:40
  1006.9 34.1 fusion.83
  1042.9 229.3 %reduce-scatter.7.cloned.1.call-done = f32[1024,2048]{1,0:T(8,128)} async-done(((f32[4096,2048]{1,0:T(8,128)}), f32[1024,2048]{1,0:T(8,128)}) %reduce-scatter.7.cloned.1.call-update) | async-done | bytes 8388624 | tf_op jit(solution)/shard_map/reduce_scatter | solution.py:69
  1272.2 1120.8 %all-reduce.14.cloned.1.call-done = f32[4096,4096]{1,0:T(8,128)} async-done(((f32[4096,4096]{1,0:T(8,128)}), f32[4096,4096]{1,0:T(8,128)}) %all-reduce.14.cloned.1.call-update) | async-done | bytes 67108880
  2415.0 298.5 %all-gather.12.cloned.1.call-done = bf16[4096,4096]{1,0:T(8,128)(2,1)} async-done(((bf16[1024,4096]{1,0:T(8,128)(2,1)}), bf16[4096,4096]{1,0:T(8,128)(2,1)}) %all-gather.12.cloned.1.call-update) | async-done | bytes 33554448 | tf_op jit(solution)/shard_map/all_gather | solution.py:73
  2738.6 290.9 %all-reduce.12.cloned.1.call-done = f32[4096,512]{1,0:T(8,128)} async-done(((f32[4096,512]{1,0:T(8,128)}), f32[4096,512]{1,0:T(8,128)}) %all-reduce.12.cloned.1.call-update) | async-done | bytes 8388624 | tf_op jit(solution)/shard_map/psum | solution.py:40
  3071.1 83.6 %reduce-scatter.9.cloned.1.call-done = f32[1024,512]{1,0:T(8,128)} async-done(((f32[4096,512]{1,0:T(8,128)}), f32[1024,512]{1,0:T(8,128)}) %reduce-scatter.9.cloned.1.call-update) | async-done | bytes 2097168 | tf_op jit(solution)/shard_map/reduce_scatter | solution.py:69
  3159.0 861.1 %while.35 = (s32[]{:T(128)}, f32[8,1024,64]{1,2,0:T(8,128)}, f32[8,8192,64]{1,2,0:T(8,128)}, f32[8,8192,64]{1,2,0:T(8,128)}, bf16[8,1024,64]{2,1,0:T(8,128)(2,1)...) while((s32[]{:T(128)}, f32[8,1024,64]{1,2,0:T(8,128)}, ...), condition=%wide.region_21.22_spmd.clone.clone, body=%wide.region_19.21_spmd.clone.sunk.clone | while | flops 5478349824 | bytes 344006528 | solution.py:224
  3178.0 28.8 multiply_reduce_fusion.6
  3206.8 27.5 multiply_convert_fusion.9
  3285.6 28.7 multiply_reduce_fusion.6
  3314.3 27.5 multiply_convert_fusion.9
  3393.1 28.7 multiply_reduce_fusion.6
  3421.8 27.5 multiply_convert_fusion.9
  3500.6 28.7 multiply_reduce_fusion.6
  3529.4 27.5 multiply_convert_fusion.9
  3608.2 28.7 multiply_reduce_fusion.6
  3637.0 27.5 multiply_convert_fusion.9
  3715.8 28.7 multiply_reduce_fusion.6
  3744.5 27.5 multiply_convert_fusion.9
  3823.3 28.7 multiply_reduce_fusion.6
  3852.1 27.5 multiply_convert_fusion.9
  3930.9 28.7 multiply_reduce_fusion.6
  3959.7 27.5 multiply_convert_fusion.9
  4039.5 46.7 reduce-scatter.11.cloned.1.call-done
  4090.9 155.2 %all-gather.10.cloned.1.call-done = bf16[4096,2048]{1,0:T(8,128)(2,1)} async-done(((bf16[1024,2048]{1,0:T(8,128)(2,1)}), bf16[4096,2048]{1,0:T(8,128)(2,1)}) %all-gather.10.cloned.1.call-update) | async-done | bytes 16777232 | tf_op jit(solution)/shard_map/all_gather | solution.py:44
  4261.0 25.4 convolution_convert_fusion
  4289.5 29.1 all-gather.14.cloned.1.call-done
  4375.6 554.8 %all-reduce.16.cloned.1.call-done = (f32[4096,512]{1,0:T(8,128)}, f32[4096,512]{1,0:T(8,128)}) async-done(((f32[4096,512]{1,0:T(8,128)}, f32[4096,512]{1,0:T(8,128)}), (f32[4096,512]{1,0:T(8,128)}, f32[4096,512]{1,0:T(8,128)})) %all-reduce.16.cloned.1.call-update) | async-done | bytes 16777232 | tf_op jit(solution)/shard_map/psum | solution.py:40
  (351 shorter events, 1176.9 us)
Async XLA Ops:
  7.2 683.1 %copy-start = (bf16[2048,512]{1,0:T(8,128)(2,1)S(1)}, bf16[2048,512]{1,0:T(8,128)(2,1)}, u32[]{:S(2)}) copy-start(bf16[2048,512]{1,0:T(8,128)(2,1)} %param.26) | copy-start | bytes 6291460
  7.2 155.2 %reduce-scatter.5.cloned.1.call-start = ((), (), s32[]{:S(2)}) async-start(), calls=%async_computation.4 | async-start | bytes 15728640 | tf_op jit(solution)/shard_map/reduce_scatter | solution.py:69
  42.1 162.9 %all-gather.6.cloned.1.call-start = ((), (), s32[]{:S(2)}) async-start(), calls=%async_computation.5 | async-start | bytes 4718592 | tf_op jit(solution)/shard_map/all_gather | solution.py:142
  43.7 124.9 %copy-start.21 = (s32[8192]{0:T(1024)S(1)}, s32[8192]{0:T(1024)}, u32[]{:S(2)}) copy-start(s32[8192]{0:T(1024)} %param.28) | copy-start | bytes 98308
  47.4 129.0 %copy-start.7 = (f32[1024,64]{0,1:T(8,128)}, f32[1024,64]{0,1:T(8,128)S(1)}, u32[]{:S(2)}) copy-start(f32[1024,64]{0,1:T(8,128)S(1)} %fusion.80) | copy-start | bytes 786436
  168.2 513.9 %all-gather.8.cloned.1.call-start = ((), (), s32[]{:S(2)}) async-start(), calls=%async_computation.6 | async-start | bytes 5242880 | tf_op jit(solution)/shard_map/all_gather | solution.py:44
  628.2 62.0 %copy-start.27 = (pred[8192]{0:T(1024)(128)(4,1)}, pred[8192]{0:T(1024)(128)(4,1)S(1)}, u32[]{:S(2)}) copy-start(pred[8192]{0:T(1024)(128)(4,1)S(1)} %get-tuple-element.864) | copy-start | bytes 24580
  628.2 62.0 %copy-start.31 = (s32[1024]{0:T(1024)}, s32[1024]{0:T(1024)S(1)}, u32[]{:S(2)}) copy-start(s32[1024]{0:T(1024)S(1)} %get-tuple-element.865) | copy-start | bytes 12292
  628.2 62.0 %copy-start.33 = (s32[1024]{0:T(1024)}, s32[1024]{0:T(1024)S(1)}, u32[]{:S(2)}) copy-start(s32[1024]{0:T(1024)S(1)} %get-tuple-element.866) | copy-start | bytes 12292
  629.1 61.1 %copy-start.22 = (s32[8192]{0:T(1024)S(1)}, s32[8192]{0:T(1024)}, u32[]{:S(2)}) copy-start(s32[8192]{0:T(1024)} %param.28) | copy-start | bytes 98308
  629.2 351.9 %all-reduce.10.cloned.1.call-start = ((), (), s32[]{:S(2)}) async-start(), calls=%async_computation.7 | async-start | bytes 16777216 | tf_op jit(solution)/shard_map/psum | solution.py:40
  690.2 582.0 %reduce-scatter.7.cloned.1.call-start = ((), (), s32[]{:S(2)}) async-start(), calls=%async_computation.9 | async-start | bytes 41943040 | tf_op jit(solution)/shard_map/reduce_scatter | solution.py:69
  690.2 2362.8 %copy-start.23 = (pred[4096]{0:T(1024)(128)(4,1)}, pred[4096]{0:T(1024)(128)(4,1)S(1)}, u32[]{:S(2)}) copy-start(pred[4096]{0:T(1024)(128)(4,1)S(1)} %dynamic-slice_compare_fusion) | copy-start | bytes 12292
  708.0 1684.9 %all-reduce.14.cloned.1.call-start = ((), (), s32[]{:S(2)}) async-start(), calls=%async_computation.15 | async-start | bytes 134217728
  714.4 292.4 %copy-start.25 = (f32[512]{0:T(512)S(1)}, f32[512]{0:T(512)}, u32[]{:S(2)}) copy-start(f32[512]{0:T(512)} %param.23) | copy-start | bytes 6148
  1006.9 2046.2 %copy-start.19 = (f32[4096]{0:T(1024)}, f32[4096]{0:T(1024)S(1)}, u32[]{:S(2)}) copy-start(f32[4096]{0:T(1024)S(1)} %add_rsqrt_fusion) | copy-start | bytes 49156
  1041.0 1672.5 %all-gather.12.cloned.1.call-start = ((), (), s32[]{:S(2)}) async-start(), calls=%async_computation.10 | async-start | bytes 41943040 | tf_op jit(solution)/shard_map/all_gather | solution.py:73
  2414.8 614.8 %all-reduce.12.cloned.1.call-start = ((), (), s32[]{:S(2)}) async-start(), calls=%async_computation.11 | async-start | bytes 16777216 | tf_op jit(solution)/shard_map/psum | solution.py:40
  2738.6 416.2 %reduce-scatter.9.cloned.1.call-start = ((), (), s32[]{:S(2)}) async-start(), calls=%async_computation.12 | async-start | bytes 10485760 | tf_op jit(solution)/shard_map/reduce_scatter | solution.py:69
  3071.0 88.0 %copy-start.16 = (s32[8192]{0:T(1024)S(1)}, s32[8192]{0:T(1024)}, u32[]{:S(2)}) copy-start(s32[8192]{0:T(1024)} %param.27) | copy-start | bytes 98308
  3071.0 88.0 %copy-start.28 = (pred[8192]{0:T(1024)(128)(4,1)S(1)}, pred[8192]{0:T(1024)(128)(4,1)}, u32[]{:S(2)}) copy-start(pred[8192]{0:T(1024)(128)(4,1)} %copy-done.27) | copy-start | bytes 24580
  3071.0 88.0 %copy-start.32 = (s32[1024]{0:T(1024)S(1)}, s32[1024]{0:T(1024)}, u32[]{:S(2)}) copy-start(s32[1024]{0:T(1024)} %copy-done.31) | copy-start | bytes 12292
  3071.0 88.0 %copy-start.34 = (s32[1024]{0:T(1024)S(1)}, s32[1024]{0:T(1024)}, u32[]{:S(2)}) copy-start(s32[1024]{0:T(1024)} %copy-done.33) | copy-start | bytes 12292
  3071.0 1015.2 %reduce-scatter.11.cloned.1.call-start = ((), (), s32[]{:S(2)}) async-start(), calls=%async_computation.13 | async-start | bytes 4718592 | tf_op jit(solution)/shard_map/reduce_scatter | solution.py:236
  4034.8 211.3 %all-gather.10.cloned.1.call-start = ((), (), s32[]{:S(2)}) async-start(), calls=%async_computation.8 | async-start | bytes 20971520 | tf_op jit(solution)/shard_map/all_gather | solution.py:44
  4035.5 283.1 %all-gather.14.cloned.1.call-start = ((), (), s32[]{:S(2)}) async-start(), calls=%async_computation.14 | async-start | bytes 7864320 | tf_op jit(solution)/shard_map/all_gather | solution.py:73
  4037.3 208.8 %copy-start.24 = (pred[4096]{0:T(1024)(128)(4,1)S(1)}, pred[4096]{0:T(1024)(128)(4,1)}, u32[]{:S(2)}) copy-start(pred[4096]{0:T(1024)(128)(4,1)} %copy-done.23) | copy-start | bytes 12292
  4090.8 170.2 %copy-start.20 = (f32[4096]{0:T(1024)S(1)}, f32[4096]{0:T(1024)}, u32[]{:S(2)}) copy-start(f32[4096]{0:T(1024)} %copy-done.19) | copy-start | bytes 49156
  4090.8 170.2 %copy-start.26 = (f32[512]{0:T(512)S(1)}, f32[512]{0:T(512)}, u32[]{:S(2)}) copy-start(f32[512]{0:T(512)} %param.23) | copy-start | bytes 6148
  4090.8 271.9 %all-reduce.18.cloned.1.call-start = ((), (), s32[]{:S(2)}) async-start(), calls=%async_computation.17 | async-start | bytes 15204352 | tf_op jit(solution)/shard_map/psum | solution.py:253
  4327.7 602.7 %all-reduce.16.cloned.1.call-start = ((), (), s32[]{:S(2)}) async-start(), calls=%async_computation.16 | async-start | bytes 33554432 | tf_op jit(solution)/shard_map/psum | solution.py:40
  4375.6 560.7 %copy-start.30 = (bf16[512]{0:T(512)(128)(2,1)S(1)}, bf16[512]{0:T(512)(128)(2,1)}, u32[]{:S(2)}) copy-start(bf16[512]{0:T(512)(128)(2,1)} %get-tuple-element.396) | copy-start | bytes 3076
  (48 other events, 629.2 us)
Sparse Core Ops, SparseCore 0:
  42.2 120.1 reduce-scatter.4
  168.3 36.6 all-gather.5
  629.3 52.7 all-gather.7
  690.2 290.8 all-reduce.9
  984.0 288.1 reduce-scatter.6
  1275.9 1116.9 all-reduce.13
  2414.9 298.5 all-gather.11
  2738.7 290.8 all-reduce.11
  3071.1 83.5 reduce-scatter.8
  4034.9 51.2 reduce-scatter.10
  4088.7 157.4 all-gather.9
  4248.4 70.1 all-gather.13
  4327.8 34.8 all-reduce.17
  4366.0 564.4 all-reduce.15
where the time goes:
time: 4990 us; the launch traced here: 4980 us
  waiting for transfers between devices  3270 us (66%)
  matrix products  1040 us (21%)
  other arithmetic  454 us (9%)
  local copies, waits for them, and re-layouts  90.9 us (2%)
  blocking collectives  68.5 us (1%)
    unnamed x15, waiting for transfers between devices  1120 us
    psum x3, waiting for transfers between devices, wide_total(): return lax.psum(values, 'wide')  1110 us
    reduce_scatter x3, waiting for transfers between devices, sum_rows(): lax.psum_scatter(term_rows(), 'narrow', scatter_dimension=0, tiled=True)  424 us
    dot_general x16, matrix products, head_scores(): lax.dot_general(query_one, key_one, (((1,), (1,)), ((), ())), preferred_e...  386 us
    all_gather x2, waiting for transfers between devices, back_rows(): shard_piece = lax.all_gather(grad_rows, 'narrow', axis=0, tiled=True)  328 us
    convert_element_type x8, other arithmetic, head_backward(): score_grad = (attn_prob * (prob_grad - inner_sum)).astype(jnp.bfloat16)  220 us
    all_gather x2, waiting for transfers between devices, gather_rows(): return lax.all_gather(values, 'narrow', axis=0, tiled=True)  208 us
    dot_general x8, matrix products, head_backward(): lax.dot_general(prob_low, grad_one, (((0,), (0,)), ((), ())), preferred_e...  119 us
  transfers between devices with their start and end apart: 14, of which 14 were waited for; matrix products, arithmetic and copies ran while one was open for 4% of the time, Pallas kernels for 0%

commit v1 on v0

--- a/solution.py
+++ b/solution.py
@@ -70,7 +70,16 @@
 
 
 def back_rows(grad_rows, weight, inputs):
-    shard_piece = lax.all_gather(grad_rows, "narrow", axis=0, tiled=True)
+    amount_of = lax.psum(1, "narrow")
+    samples = [(q, (q + 1) % amount_of) for q in range(amount_of)]
+    heap = [(q, (q - 1) % amount_of) for q in range(amount_of)]
+    passed, seen_now = ([grad_rows], [grad_rows])
+    for _ in range(amount_of // 2):
+        passed.append(lax.ppermute(passed[-1], "narrow", samples))
+    for _ in range((amount_of - 1) // 2):
+        seen_now.append(lax.ppermute(seen_now[-1], "narrow", heap))
+    t1 = jnp.concatenate([*passed[::-1], *seen_now[1:]], 0)
+    shard_piece = jnp.roll(t1, (lax.axis_index("narrow") - amount_of // 2) * grad_rows.shape[0], 0)
     product = lax.dot_general(
         shard_piece, weight, (((1,), (1,)), ((), ())), preferred_element_type=jnp.float32
     )

time: 4990 us -> 5320 us (1.066)
  waiting for transfers between devices: 3270 us -> 3520 us
  local copies, waits for them, and re-layouts: 90.9 us -> 152 us
    ppermute x0 -> x6, waiting for transfers between devices: none -> 552 us  [the longest x4 398 us: back_rows(): passed.append(lax.ppermute(passed[-1], 'narrow', samples))]
    all_gather x2 -> x0, waiting for transfers between devices: 328 us -> none  [back_rows(): shard_piece = lax.all_gather(grad_rows, 'narrow', axis=0, tiled=True)]
    unnamed x15 -> x13, waiting for transfers between devices: 1120 us -> 1120 us
  transfers between devices with their start and end apart: 14 -> 18, of which waited for: 14 -> 16; matrix products, arithmetic and copies ran while one was open for 4% -> 4% of each run, Pallas kernels for 0% -> 0%
where the time goes in v1:
time: 5320 us; the launch traced here: 5310 us
  waiting for transfers between devices  3520 us (66%)
  matrix products  1040 us (20%)
  other arithmetic  470 us (9%)
  local copies, waits for them, and re-layouts  152 us (3%)
  blocking collectives  68.6 us (1%)
    unnamed x13, waiting for transfers between devices  1120 us
    psum x3, waiting for transfers between devices, wide_total(): return lax.psum(values, 'wide')  1110 us
    reduce_scatter x3, waiting for transfers between devices, sum_rows(): lax.psum_scatter(term_rows(), 'narrow', scatter_dimension=0, tiled=True)  424 us
    ppermute x4, waiting for transfers between devices, back_rows(): passed.append(lax.ppermute(passed[-1], 'narrow', samples))  398 us
    dot_general x16, matrix products, head_scores(): lax.dot_general(query_one, key_one, (((1,), (1,)), ((), ())), preferred_e...  387 us
    all_gather x2, waiting for transfers between devices, gather_rows(): return lax.all_gather(values, 'narrow', axis=0, tiled=True)  227 us
    convert_element_type x8, other arithmetic, head_backward(): score_grad = (attn_prob * (prob_grad - inner_sum)).astype(jnp.bfloat16)  220 us
    ppermute x2, waiting for transfers between devices, back_rows(): seen_now.append(lax.ppermute(seen_now[-1], 'narrow', heap))  155 us
  transfers between devices with their start and end apart: 18, of which 16 were waited for; matrix products, arithmetic and copies ran while one was open for 4% of the time, Pallas kernels for 0%

profile of v1, /device:TPU:0, one launch (start us, length us, event | category | flops | bytes accessed | tf_op | source)
XLA Modules:
  0.0 5312.7 jit_solution(16041763502802789868)
XLA Ops:
  51.3 111.1 %reduce-scatter.5.cloned.1.call-done = f32[1024,768]{1,0:T(8,128)} async-done(((f32[4096,768]{1,0:T(8,128)}), f32[1024,768]{1,0:T(8,128)}) %reduce-scatter.5.cloned.1.call-update) | async-done | bytes 3145744 | tf_op jit(solution)/shard_map/reduce_scatter | solution.py:69
  217.7 410.7 %while.34 = (s32[]{:T(128)}, bf16[8,1024,64]{1,2,0:T(8,128)(2,1)S(1)}, f32[8,1024]{1,0:T(8,128)}, bf16[8,1024,64]{2,1,0:T(8,128)(2,1)}, s32[8]{0:T(128)S(1)}, /*...) while((s32[]{:T(128)}, ...), condition=%wide.region_8.9_spmd.clone.clone, body=%wide.region_5.8_spmd.clone.sunk.clone | while | flops 2239757312 | bytes 111760208 | solution.py:177
  629.6 52.6 all-gather.6.cloned.1.call-done
  715.2 266.2 %all-reduce.10.cloned.1.call-done = f32[4096,512]{1,0:T(8,128)} async-done(((f32[4096,512]{1,0:T(8,128)}), f32[4096,512]{1,0:T(8,128)}) %all-reduce.10.cloned.1.call-update) | async-done | bytes 8388624 | tf_op jit(solution)/shard_map/psum | solution.py:40
  1007.2 34.1 fusion.101
  1043.2 229.2 %reduce-scatter.7.cloned.1.call-done = f32[1024,2048]{1,0:T(8,128)} async-done(((f32[4096,2048]{1,0:T(8,128)}), f32[1024,2048]{1,0:T(8,128)}) %reduce-scatter.7.cloned.1.call-update) | async-done | bytes 8388624 | tf_op jit(solution)/shard_map/reduce_scatter | solution.py:69
  1272.4 1120.8 %all-reduce.14.cloned.1.call-done = f32[4096,4096]{1,0:T(8,128)} async-done(((f32[4096,4096]{1,0:T(8,128)}), f32[4096,4096]{1,0:T(8,128)}) %all-reduce.14.cloned.1.call-update) | async-done | bytes 67108880
  2416.5 182.2 %collective-permute-done = bf16[1024,4096]{1,0:T(8,128)(2,1)} collective-permute-done((bf16[1024,4096]{1,0:T(8,128)(2,1)}, bf16[1024,4096]{1,0:T(8,128)(2,1)}, u32[]{:S(2)}, u32[]{:S(2)}) %collective-permute-start) | collective-permute-done | bytes 8388640 | tf_op jit(solution)/shard_map/ppermute | solution.py:78
  2602.0 181.2 %collective-permute-done.1 = bf16[1024,4096]{1,0:T(8,128)(2,1)} collective-permute-done((bf16[1024,4096]{1,0:T(8,128)(2,1)}, bf16[1024,4096]{1,0:T(8,128)(2,1)}, u32[]{:S(2)}, u32[]{:S(2)}) %collective-permute-start.1) | collective-permute-done | bytes 8388640 | tf_op jit(solution)/shard_map/ppermute | solution.py:78
  2806.6 154.7 %collective-permute-done.2 = bf16[1024,4096]{1,0:T(8,128)(2,1)} collective-permute-done((bf16[1024,4096]{1,0:T(8,128)(2,1)}, bf16[1024,4096]{1,0:T(8,128)(2,1)}, u32[]{:S(2)}, u32[]{:S(2)}) %collective-permute-start.2) | collective-permute-done | bytes 8388640 | tf_op jit(solution)/shard_map/ppermute | solution.py:80
  3025.1 289.9 %all-reduce.12.cloned.1.call-done = f32[4096,512]{1,0:T(8,128)} async-done(((f32[4096,512]{1,0:T(8,128)}), f32[4096,512]{1,0:T(8,128)}) %all-reduce.12.cloned.1.call-update) | async-done | bytes 8388624 | tf_op jit(solution)/shard_map/psum | solution.py:40
  3356.6 83.6 %reduce-scatter.9.cloned.1.call-done = f32[1024,512]{1,0:T(8,128)} async-done(((f32[4096,512]{1,0:T(8,128)}), f32[1024,512]{1,0:T(8,128)}) %reduce-scatter.9.cloned.1.call-update) | async-done | bytes 2097168 | tf_op jit(solution)/shard_map/reduce_scatter | solution.py:69
  3444.5 861.2 %while.35 = (s32[]{:T(128)}, f32[8,1024,64]{1,2,0:T(8,128)}, f32[8,8192,64]{1,2,0:T(8,128)}, f32[8,8192,64]{1,2,0:T(8,128)}, bf16[8,1024,64]{2,1,0:T(8,128)(2,1)...) while((s32[]{:T(128)}, f32[8,1024,64]{1,2,0:T(8,128)}, ...), condition=%wide.region_21.22_spmd.clone.clone, body=%wide.region_19.21_spmd.clone.sunk.clone | while | flops 5478349824 | bytes 344006528 | solution.py:233
  3463.1 28.8 multiply_reduce_fusion.6
  3491.9 27.5 multiply_convert_fusion.9
  3570.7 28.8 multiply_reduce_fusion.6
  3599.5 27.5 multiply_convert_fusion.9
  3678.2 28.8 multiply_reduce_fusion.6
  3707.1 27.5 multiply_convert_fusion.9
  3785.8 28.8 multiply_reduce_fusion.6
  3814.6 27.5 multiply_convert_fusion.9
  3893.4 28.8 multiply_reduce_fusion.6
  4001.0 28.8 multiply_reduce_fusion.6
  4108.6 28.8 multiply_reduce_fusion.6
  4137.5 27.5 multiply_convert_fusion.9
  4216.2 28.8 multiply_reduce_fusion.6
  4245.0 27.5 multiply_convert_fusion.9
  4325.0 46.9 reduce-scatter.11.cloned.1.call-done
  4377.9 27.6 fusion.67
  4406.3 34.2 collective-permute-done.3
  4442.1 174.2 %all-gather.8.cloned.1.call-done = bf16[4096,2048]{1,0:T(8,128)(2,1)} async-done(((bf16[1024,2048]{1,0:T(8,128)(2,1)}), bf16[4096,2048]{1,0:T(8,128)(2,1)}) %all-gather.8.cloned.1.call-update) | async-done | bytes 16777232 | tf_op jit(solution)/shard_map/all_gather | solution.py:44
  4704.6 554.8 %all-reduce.16.cloned.1.call-done = (f32[4096,512]{1,0:T(8,128)}, f32[4096,512]{1,0:T(8,128)}) async-done(((f32[4096,512]{1,0:T(8,128)}, f32[4096,512]{1,0:T(8,128)}), (f32[4096,512]{1,0:T(8,128)}, f32[4096,512]{1,0:T(8,128)})) %all-reduce.16.cloned.1.call-update) | async-done | bytes 16777232 | tf_op jit(solution)/shard_map/psum | solution.py:40
  (384 shorter events, 1315.2 us)
Async XLA Ops:
  7.2 683.9 %copy-start = (bf16[2048,512]{1,0:T(8,128)(2,1)S(1)}, bf16[2048,512]{1,0:T(8,128)(2,1)}, u32[]{:S(2)}) copy-start(bf16[2048,512]{1,0:T(8,128)(2,1)} %param.26) | copy-start | bytes 6291460
  7.2 155.2 %reduce-scatter.5.cloned.1.call-start = ((), (), s32[]{:S(2)}) async-start(), calls=%async_computation.4 | async-start | bytes 15728640 | tf_op jit(solution)/shard_map/reduce_scatter | solution.py:69
  42.1 162.9 %all-gather.4.cloned.1.call-start = ((), (), s32[]{:S(2)}) async-start(), calls=%async_computation.5 | async-start | bytes 4718592 | tf_op jit(solution)/shard_map/all_gather | solution.py:151
  43.7 125.2 %copy-start.28 = (s32[8192]{0:T(1024)S(1)}, s32[8192]{0:T(1024)}, u32[]{:S(2)}) copy-start(s32[8192]{0:T(1024)} %param.28) | copy-start | bytes 98308
  47.4 129.3 %copy-start.8 = (f32[1024,64]{0,1:T(8,128)}, f32[1024,64]{0,1:T(8,128)S(1)}, u32[]{:S(2)}) copy-start(f32[1024,64]{0,1:T(8,128)S(1)} %fusion.94) | copy-start | bytes 786436
  168.1 514.1 %all-gather.6.cloned.1.call-start = ((), (), s32[]{:S(2)}) async-start(), calls=%async_computation.6 | async-start | bytes 5242880 | tf_op jit(solution)/shard_map/all_gather | solution.py:44
  628.4 62.0 %copy-start.39 = (s32[1024]{0:T(1024)}, s32[1024]{0:T(1024)S(1)}, u32[]{:S(2)}) copy-start(s32[1024]{0:T(1024)S(1)} %get-tuple-element.861) | copy-start | bytes 12292
  628.4 62.0 %copy-start.41 = (s32[1024]{0:T(1024)}, s32[1024]{0:T(1024)S(1)}, u32[]{:S(2)}) copy-start(s32[1024]{0:T(1024)S(1)} %get-tuple-element.862) | copy-start | bytes 12292
  629.4 351.9 %all-reduce.10.cloned.1.call-start = ((), (), s32[]{:S(2)}) async-start(), calls=%async_computation.7 | async-start | bytes 16777216 | tf_op jit(solution)/shard_map/psum | solution.py:40
  690.4 582.0 %reduce-scatter.7.cloned.1.call-start = ((), (), s32[]{:S(2)}) async-start(), calls=%async_computation.9 | async-start | bytes 41943040 | tf_op jit(solution)/shard_map/reduce_scatter | solution.py:69
  708.8 1684.4 %all-reduce.14.cloned.1.call-start = ((), (), s32[]{:S(2)}) async-start(), calls=%async_computation.13 | async-start | bytes 134217728
  715.2 292.0 %copy-start.33 = (f32[512]{0:T(512)S(1)}, f32[512]{0:T(512)}, u32[]{:S(2)}) copy-start(f32[512]{0:T(512)} %param.23) | copy-start | bytes 6148
  1007.2 2331.4 %copy-start.26 = (f32[4096]{0:T(1024)}, f32[4096]{0:T(1024)S(1)}, u32[]{:S(2)}) copy-start(f32[4096]{0:T(1024)S(1)} %add_rsqrt_fusion) | copy-start | bytes 49156
  1041.4 2273.7 %all-reduce.12.cloned.1.call-start = ((), (), s32[]{:S(2)}) async-start(), calls=%async_computation.10 | async-start | bytes 16777216 | tf_op jit(solution)/shard_map/psum | solution.py:40
  2415.0 183.6 %collective-permute-start = (bf16[1024,4096]{1,0:T(8,128)(2,1)}, bf16[1024,4096]{1,0:T(8,128)(2,1)}, u32[]{:S(2)}, u32[]{:S(2)}) collective-permute-start(bf16[1024,4096]{1,0:T(8,128)(2,1)} %pad_maximum_fusion), channel_id=1, source_target_pairs={{0,4},{4,8},{8,12},{12,0},{1,5},{5,9},{9,13},{13,1},{2,6},{6,10},{... | collective-permute-start | bytes 25165832 | tf_op jit(solution)/shard_map/ppermute | solution.py:78
  2598.6 184.6 %collective-permute-start.1 = (bf16[1024,4096]{1,0:T(8,128)(2,1)}, bf16[1024,4096]{1,0:T(8,128)(2,1)}, u32[]{:S(2)}, u32[]{:S(2)}) collective-permute-start(bf16[1024,4096]{1,0:T(8,128)(2,1)} %collective-permute-done), channel_id=1, source_target_pairs={{0,4},{4,8},{8,12},{12,0},{1,5},{5,9},{9,13},{13,1},{2,6},{6,10},{... | collective-permute-start | bytes 25165832 | tf_op jit(solution)/shard_map/ppermute | solution.py:78
  2599.1 362.2 %collective-permute-start.2 = (bf16[1024,4096]{1,0:T(8,128)(2,1)}, bf16[1024,4096]{1,0:T(8,128)(2,1)}, u32[]{:S(2)}, u32[]{:S(2)}) collective-permute-start(bf16[1024,4096]{1,0:T(8,128)(2,1)} %pad_maximum_fusion), channel_id=1, source_target_pairs={{0,12},{4,0},{8,4},{12,8},{1,13},{5,1},{9,5},{13,9},{2,14},{6,2},{... | collective-permute-start | bytes 25165832 | tf_op jit(solution)/shard_map/ppermute | solution.py:80
  3025.1 313.5 %copy-start.31 = (pred[4096]{0:T(1024)(128)(4,1)S(1)}, pred[4096]{0:T(1024)(128)(4,1)}, u32[]{:S(2)}) copy-start(pred[4096]{0:T(1024)(128)(4,1)} %copy-done.30) | copy-start | bytes 12292
  3025.1 415.2 %reduce-scatter.9.cloned.1.call-start = ((), (), s32[]{:S(2)}) async-start(), calls=%async_computation.11 | async-start | bytes 10485760 | tf_op jit(solution)/shard_map/reduce_scatter | solution.py:69
  3356.5 88.0 %copy-start.23 = (s32[8192]{0:T(1024)S(1)}, s32[8192]{0:T(1024)}, u32[]{:S(2)}) copy-start(s32[8192]{0:T(1024)} %param.27) | copy-start | bytes 98308
  3356.5 88.0 %copy-start.36 = (pred[8192]{0:T(1024)(128)(4,1)S(1)}, pred[8192]{0:T(1024)(128)(4,1)}, u32[]{:S(2)}) copy-start(pred[8192]{0:T(1024)(128)(4,1)} %copy-done.35) | copy-start | bytes 24580
  3356.5 88.0 %copy-start.40 = (s32[1024]{0:T(1024)S(1)}, s32[1024]{0:T(1024)}, u32[]{:S(2)}) copy-start(s32[1024]{0:T(1024)} %copy-done.39) | copy-start | bytes 12292
  3356.5 88.0 %copy-start.42 = (s32[1024]{0:T(1024)S(1)}, s32[1024]{0:T(1024)}, u32[]{:S(2)}) copy-start(s32[1024]{0:T(1024)} %copy-done.41) | copy-start | bytes 12292
  3356.5 1015.3 %reduce-scatter.11.cloned.1.call-start = ((), (), s32[]{:S(2)}) async-start(), calls=%async_computation.12 | async-start | bytes 4718592 | tf_op jit(solution)/shard_map/reduce_scatter | solution.py:245
  4320.4 295.9 %all-gather.8.cloned.1.call-start = ((), (), s32[]{:S(2)}) async-start(), calls=%async_computation.8 | async-start | bytes 20971520 | tf_op jit(solution)/shard_map/all_gather | solution.py:44
  4320.9 370.7 %all-reduce.18.cloned.1.call-start = ((), (), s32[]{:S(2)}) async-start(), calls=%async_computation.15 | async-start | bytes 15204352 | tf_op jit(solution)/shard_map/psum | solution.py:262
  4376.5 239.8 %copy-start.32 = (pred[4096]{0:T(1024)(128)(4,1)S(1)}, pred[4096]{0:T(1024)(128)(4,1)}, u32[]{:S(2)}) copy-start(pred[4096]{0:T(1024)(128)(4,1)} %copy-done.30) | copy-start | bytes 12292
  4376.5 64.0 %collective-permute-start.3 = (bf16[1024,768]{0,1:T(8,128)(2,1)}, bf16[1024,768]{0,1:T(8,128)(2,1)}, u32[]{:S(2)}, u32[]{:S(2)}) collective-permute-start(bf16[1024,768]{0,1:T(8,128)(2,1)} %pad_maximum_fusion.2), channel_id=1, source_target_pairs={{0,4},{4,8},{8,12},{12,0},{1,5},{5,9},{9,13},{13,1},{2,6},{6,10},{... | collective-permute-start | bytes 4718600 | tf_op jit(solution)/shard_map/ppermute | solution.py:78
  4405.5 235.6 %collective-permute-start.5 = (bf16[1024,768]{0,1:T(8,128)(2,1)}, bf16[1024,768]{0,1:T(8,128)(2,1)}, u32[]{:S(2)}, u32[]{:S(2)}) collective-permute-start(bf16[1024,768]{0,1:T(8,128)(2,1)} %pad_maximum_fusion.2), channel_id=1, source_target_pairs={{0,12},{4,0},{8,4},{12,8},{1,13},{5,1},{9,5},{13,9},{2,14},{6,2},{... | collective-permute-start | bytes 4718600 | tf_op jit(solution)/shard_map/ppermute | solution.py:80
  4440.4 197.3 %collective-permute-start.4 = (bf16[1024,768]{0,1:T(8,128)(2,1)}, bf16[1024,768]{0,1:T(8,128)(2,1)}, u32[]{:S(2)}, u32[]{:S(2)}) collective-permute-start(bf16[1024,768]{0,1:T(8,128)(2,1)} %collective-permute-done.3), channel_id=1, source_target_pairs={{0,4},{4,8},{8,12},{12,0},{1,5},{5,9},{9,13},{13,1},{2,6},{6,10},{... | collective-permute-start | bytes 4718600 | tf_op jit(solution)/shard_map/ppermute | solution.py:78
  4657.5 601.9 %all-reduce.16.cloned.1.call-start = ((), (), s32[]{:S(2)}) async-start(), calls=%async_computation.14 | async-start | bytes 33554432 | tf_op jit(solution)/shard_map/psum | solution.py:40
  4704.6 560.7 %copy-start.38 = (bf16[512]{0:T(512)(128)(2,1)S(1)}, bf16[512]{0:T(512)(128)(2,1)}, u32[]{:S(2)}) copy-start(bf16[512]{0:T(512)(128)(2,1)} %get-tuple-element.396) | copy-start | bytes 3076
  (58 other events, 800.8 us)
Sparse Core Ops, SparseCore 0:
  42.2 120.1 reduce-scatter.4
  168.3 36.6 all-gather.3
  629.5 52.6 all-gather.5
  690.5 290.8 all-reduce.9
  984.3 288.1 reduce-scatter.6
  1276.2 1116.9 all-reduce.13
  3025.2 289.8 all-reduce.11
  3356.6 83.5 reduce-scatter.8
  4320.5 51.3 reduce-scatter.10
  4374.1 242.0 all-gather.7
  4657.6 34.0 all-reduce.17
  4694.9 564.4 all-reduce.15
